TPU v7x, 256 devices: a whole 4x4x8 slice. The times are simulated.
256 devices in a mesh: pipe: 16 (over z, core), dp: 4 (over x), tensor: 4 (over y).
Axes of the slice: x: 4, y: 4, z: 8, core: 2. Of those that a mesh axis runs over, the one named last changes fastest.
Arguments:
- acts: bfloat16 [16, 2048, 8192], P('pipe', 'dp', 'tensor'), may hold values from -6 to 6
- grads: bfloat16 [16, 2048, 8192], P('pipe', 'dp', 'tensor'), may hold values from -6 to 6
- sketch_index: int32 [16, 2, 16], P('pipe'), may hold values from 0 to 63, as said below
- sketch_values: bfloat16 [16, 2, 16, 128, 32], P('pipe'), may hold values from -0.125 to 0.125
Outputs:
- basis: float32 [16384, 256], P(('pipe', 'tensor'), 'dp')
Inputs may be any that keep to these rules, and one draw needn't show every extreme that they name: `sketch_index`: the 16 blocks of each sketch are distinct.
All inputs are finite; a program needn't handle non-finite values.
Results may differ from a plain program's by a relative error of at most 0.0003.
Values sent between devices are 32-bit elements; how exact they have to be, the bound alone decides.
A program may use at most 64 MiB of HBM per device.

v0:
```python
import jax
import jax.numpy as jnp
from jax import lax
from jax.sharding import PartitionSpec as P

RANK = 256
ITERS = 2
TOK_EX = 4


def from_partner(block, axis, apart):
    count = lax.axis_size(axis)
    route = []
    for low in range(count):
        high = low | 1 << apart
        if high != low and high < count:
            route += [(low, high), (high, low)]
    return lax.ppermute(block, axis, route)


def mm(a, b):
    return jnp.matmul(a, b, precision=lax.Precision.HIGHEST)


def layer_total(value):
    return lax.psum(value, "pipe")


def orthonormal(block, total):
    lower = jnp.linalg.cholesky(total(mm(block.T, block)))
    return lax.linalg.triangular_solve(lower, block, left_side=False, lower=True, transpose_a=True)


def reduce_plain(joined, total):
    q_basis = orthonormal(joined[:, :RANK] + joined[:, RANK:], total)
    for turn in range(ITERS):
        q_basis = orthonormal(mm(joined, total(mm(joined.T, q_basis))), total)
    weights = total(mm(joined.T, q_basis))
    lower = jnp.linalg.cholesky(mm(weights.T, weights))
    return mm(q_basis, lower)


def shards(acts, grads, sketch_index, sketch_values):
    local_width = acts.shape[2]
    blocks = local_width // 128
    width = sketch_values.shape[4]
    tensor_pos = lax.axis_index("tensor")
    tensor_count = lax.axis_size("tensor")
    span = jnp.arange(blocks, dtype=jnp.int32) + tensor_pos * blocks
    onehot = (sketch_index[0][:, :, None] == span[None, None, :]).astype(jnp.bfloat16)
    local = jnp.einsum(
        "sij,sicd->sjcd", onehot, sketch_values[0], preferred_element_type=jnp.float32
    )
    local = local.astype(jnp.bfloat16).reshape(2, local_width, width)
    left_part = jnp.dot(acts[0], local[0], preferred_element_type=jnp.float32)
    right_part = jnp.dot(grads[0], local[1], preferred_element_type=jnp.float32)
    both = lax.psum(jnp.concatenate([left_part, right_part], axis=1), "tensor")
    left_all = both[:, :width].reshape(-1, TOK_EX, width)
    right_all = both[:, width:].reshape(-1, TOK_EX, width)
    outer = jnp.einsum("etk,etl->ekl", left_all, right_all, precision=lax.Precision.HIGHEST)
    current = outer.reshape(outer.shape[0], -1).T
    position = lax.axis_index("dp")
    for bit in range(lax.axis_size("dp").bit_length() - 1):
        partner = from_partner(current, "dp", bit)
        upper = jnp.right_shift(position, bit) % 2
        joined = jnp.where(
            upper == 0,
            jnp.concatenate([current, partner], axis=1),
            jnp.concatenate([partner, current], axis=1),
        )
        if joined.shape[1] <= RANK:
            current = joined
        else:
            current = reduce_plain(joined, layer_total)
    part_rows = current.shape[0] // tensor_count
    current = lax.dynamic_slice_in_dim(current, tensor_pos * part_rows, part_rows, 0)
    own_columns = current.shape[1] // lax.axis_size("dp")
    current = lax.dynamic_slice_in_dim(current, position * own_columns, own_columns, 1)
    return current


def solution(mesh):
    placed = (
        P("pipe", "dp", "tensor"),
        P("pipe", "dp", "tensor"),
        P("pipe", None, None),
        P("pipe", None, None, None, None),
    )
    return jax.shard_map(
        shards, mesh=mesh, in_specs=placed, out_specs=P(("pipe", "tensor"), "dp"), check_vma=False
    )
```

profile of v0, /device:TPU:1, one launch (start us, length us, event | category | flops | bytes accessed | tf_op | source)
XLA Modules:
  0.0 1064.1 jit_solution(16470218660606452282)
XLA Ops:
  10.4 48.4 %all-reduce.9.cloned.1.call-done = f32[512,64]{0,1:T(8,128)} async-done(((f32[512,64]{0,1:T(8,128)}), f32[512,64]{0,1:T(8,128)}) %all-reduce.9.cloned.1.call-update) | async-done | bytes 131088 | tf_op jit(solution)/shard_map/psum | solution.py:57
  60.0 4.8 fusion.84
  68.7 9.7 collective-permute-done
  82.8 20.0 %collective-permute-done.1 = f32[1024,256]{1,0:T(8,128)} collective-permute-done((f32[1024,256]{1,0:T(8,128)S(1)}, f32[1024,256]{1,0:T(8,128)}, u32[]{:S(2)}, u32[]{:S(2)}) %collective-permute-start.1) | collective-permute-done | bytes 1048608 | tf_op jit(solution)/shard_map/ppermute | solution.py:18
  109.0 114.7 %all-reduce.11.cloned.1.call-done = f32[256,256]{0,1:T(8,128)} async-done(((f32[256,256]{0,1:T(8,128)}), f32[256,256]{0,1:T(8,128)}) %all-reduce.11.cloned.1.call-update) | async-done | bytes 262160 | tf_op jit(solution)/shard_map/psum | solution.py:26
  226.5 11.7 %cholesky.214 = f32[128,128]{1,0:T(8,128)S(1)} custom-call(f32[128,128]{1,0:T(8,128)S(1)} %cholesky.346), custom_call_target="Cholesky" | custom-call | tf_op jit(solution)/shard_map/jit(cholesky)/cholesky | solution.py:30
  238.2 9.8 custom-call.16
  250.2 11.7 %cholesky.231 = f32[128,128]{1,0:T(8,128)S(1)} custom-call(f32[128,128]{1,0:T(8,128)S(1)} %convolution_subtract_fusion.3), custom_call_target="Cholesky" | custom-call | tf_op jit(solution)/shard_map/jit(cholesky)/cholesky | solution.py:30
  264.9 4.1 while.6
  269.6 20.5 %custom-call.17 = f32[2,128,128]{1,2,0:T(8,128)S(1)} custom-call(f32[2,128,128]{2,1,0:T(8,128)} %copy-done.18), custom_call_target="InvertDiagBlocksLowerTriangular" | custom-call | tf_op jit(solution)/shard_map/triangular_solve/custom-call.0 | solution.py:31
  292.5 4.3 fusion.10
  296.8 111.3 %all-reduce.13.cloned.1.call-done = f32[512,256]{1,0:T(8,128)} async-done(((f32[512,256]{1,0:T(8,128)}), f32[512,256]{1,0:T(8,128)}) %all-reduce.13.cloned.1.call-update) | async-done | bytes 524304 | tf_op jit(solution)/shard_map/psum | solution.py:26
  414.6 110.1 %all-reduce.15.cloned.1.call-done = f32[256,256]{0,1:T(8,128)} async-done(((f32[256,256]{0,1:T(8,128)}), f32[256,256]{0,1:T(8,128)}) %all-reduce.15.cloned.1.call-update) | async-done | bytes 262160 | tf_op jit(solution)/shard_map/psum | solution.py:26
  527.5 11.7 %cholesky.248 = f32[128,128]{1,0:T(8,128)S(1)} custom-call(f32[128,128]{1,0:T(8,128)S(1)} %cholesky.349), custom_call_target="Cholesky" | custom-call | tf_op jit(solution)/shard_map/jit(cholesky)/cholesky | solution.py:30
  539.3 9.8 custom-call.18
  551.3 11.7 %cholesky.265 = f32[128,128]{1,0:T(8,128)S(1)} custom-call(f32[128,128]{1,0:T(8,128)S(1)} %convolution_subtract_fusion.2), custom_call_target="Cholesky" | custom-call | tf_op jit(solution)/shard_map/jit(cholesky)/cholesky | solution.py:30
  566.5 4.1 while.7
  571.2 20.5 %custom-call.19 = f32[2,128,128]{1,2,0:T(8,128)S(1)} custom-call(f32[2,128,128]{2,1,0:T(8,128)} %copy-done.19), custom_call_target="InvertDiagBlocksLowerTriangular" | custom-call | tf_op jit(solution)/shard_map/triangular_solve/custom-call.0 | solution.py:31
  594.1 4.3 fusion.14
  598.4 111.3 %all-reduce.17.cloned.1.call-done = f32[512,256]{1,0:T(8,128)} async-done(((f32[512,256]{1,0:T(8,128)}), f32[512,256]{1,0:T(8,128)}) %all-reduce.17.cloned.1.call-update) | async-done | bytes 524304 | tf_op jit(solution)/shard_map/psum | solution.py:26
  709.7 3.5 fusion.88
  716.2 110.1 %all-reduce.19.cloned.1.call-done = f32[256,256]{0,1:T(8,128)} async-done(((f32[256,256]{0,1:T(8,128)}), f32[256,256]{0,1:T(8,128)}) %all-reduce.19.cloned.1.call-update) | async-done | bytes 262160 | tf_op jit(solution)/shard_map/psum | solution.py:26
  829.1 11.7 %cholesky.282 = f32[128,128]{1,0:T(8,128)S(1)} custom-call(f32[128,128]{1,0:T(8,128)S(1)} %cholesky.352), custom_call_target="Cholesky" | custom-call | tf_op jit(solution)/shard_map/jit(cholesky)/cholesky | solution.py:30
  840.9 9.8 custom-call.20
  852.9 11.7 %cholesky.299 = f32[128,128]{1,0:T(8,128)S(1)} custom-call(f32[128,128]{1,0:T(8,128)S(1)} %convolution_subtract_fusion.1), custom_call_target="Cholesky" | custom-call | tf_op jit(solution)/shard_map/jit(cholesky)/cholesky | solution.py:30
  868.1 3.9 while.8
  872.6 20.7 %custom-call.21 = f32[2,128,128]{1,2,0:T(8,128)S(1)} custom-call(f32[2,128,128]{2,1,0:T(8,128)} %copy-done.20), custom_call_target="InvertDiagBlocksLowerTriangular" | custom-call | tf_op jit(solution)/shard_map/triangular_solve/custom-call.0 | solution.py:31
  896.4 4.3 fusion.19
  900.8 111.3 %all-reduce.21.cloned.1.call-done = f32[512,256]{1,0:T(8,128)} async-done(((f32[512,256]{1,0:T(8,128)}), f32[512,256]{1,0:T(8,128)}) %all-reduce.21.cloned.1.call-update) | async-done | bytes 524304 | tf_op jit(solution)/shard_map/psum | solution.py:26
  1016.8 11.7 %cholesky.316 = f32[128,128]{1,0:T(8,128)S(1)} custom-call(f32[128,128]{1,0:T(8,128)S(1)} %cholesky.355), custom_call_target="Cholesky" | custom-call | tf_op jit(solution)/shard_map/jit(cholesky)/cholesky | solution.py:39
  1028.6 10.0 custom-call.22
  1040.7 11.7 %cholesky.333 = f32[128,128]{1,0:T(8,128)S(1)} custom-call(f32[128,128]{1,0:T(8,128)S(1)} %convolution_subtract_fusion), custom_call_target="Cholesky" | custom-call | tf_op jit(solution)/shard_map/jit(cholesky)/cholesky | solution.py:39
  (152 shorter events, 81.6 us)
Async XLA Ops:
  6.5 1.7 copy-start
  6.5 52.3 %all-reduce.9.cloned.1.call-start = ((), (), s32[]{:S(2)}) async-start(), calls=%async_computation | async-start | bytes 262144 | tf_op jit(solution)/shard_map/psum | solution.py:57
  6.5 2.4 copy-start.10
  10.4 213.3 %all-reduce.11.cloned.1.call-start = ((), (), s32[]{:S(2)}) async-start(), calls=%async_computation.1 | async-start | bytes 524288 | tf_op jit(solution)/shard_map/psum | solution.py:26
  67.5 1.3 copy-start.9
  67.5 10.9 %collective-permute-start = (f32[1024,128]{1,0:T(8,128)S(1)}, f32[1024,128]{1,0:T(8,128)}, u32[]{:S(2)}, u32[]{:S(2)}) collective-permute-start(f32[1024,128]{1,0:T(8,128)S(1)} %bitcast.167), channel_id=1, source_target_pairs={{0,4},{4,0},{8,12},{12,8},{1,5},{5,1},{9,13},{13,9},{2,6},{6,2},{1... | collective-permute-start | bytes 1572872 | tf_op jit(solution)/shard_map/ppermute | solution.py:18
  80.0 22.8 %collective-permute-start.1 = (f32[1024,256]{1,0:T(8,128)S(1)}, f32[1024,256]{1,0:T(8,128)}, u32[]{:S(2)}, u32[]{:S(2)}) collective-permute-start(f32[1024,256]{1,0:T(8,128)S(1)} %maximum_select_fusion.1), channel_id=1, source_target_pairs={{0,8},{8,0},{4,12},{12,4},{1,9},{9,1},{5,13},{13,5},{2,10},{10,2},... | collective-permute-start | bytes 3145736 | tf_op jit(solution)/shard_map/ppermute | solution.py:18
  104.8 1.4 copy-start.1
  108.8 299.3 %all-reduce.13.cloned.1.call-start = ((), (), s32[]{:S(2)}) async-start(), calls=%async_computation.2 | async-start | bytes 1048576 | tf_op jit(solution)/shard_map/psum | solution.py:26
  225.7 0.7 copy-start.15
  262.0 1.8 copy-start.11
  269.0 0.7 copy-start.18
  290.1 2.3 copy-start.2
  296.8 228.0 %all-reduce.15.cloned.1.call-start = ((), (), s32[]{:S(2)}) async-start(), calls=%async_computation.3 | async-start | bytes 524288 | tf_op jit(solution)/shard_map/psum | solution.py:26
  414.1 295.6 %all-reduce.17.cloned.1.call-start = ((), (), s32[]{:S(2)}) async-start(), calls=%async_computation.4 | async-start | bytes 1048576 | tf_op jit(solution)/shard_map/psum | solution.py:26
  526.8 0.7 copy-start.16
  563.0 2.5 copy-start.12
  570.6 0.7 copy-start.19
  591.7 2.3 copy-start.3
  598.4 227.9 %all-reduce.19.cloned.1.call-start = ((), (), s32[]{:S(2)}) async-start(), calls=%async_computation.5 | async-start | bytes 524288 | tf_op jit(solution)/shard_map/psum | solution.py:26
  715.7 296.4 %all-reduce.21.cloned.1.call-start = ((), (), s32[]{:S(2)}) async-start(), calls=%async_computation.6 | async-start | bytes 1048576 | tf_op jit(solution)/shard_map/psum | solution.py:26
  828.4 0.7 copy-start.17
  864.6 2.5 copy-start.13
  872.0 0.7 copy-start.20
  893.3 3.1 copy-start.4
  894.0 1.7 copy-start.5
  895.6 0.8 copy-start.7
  900.7 154.5 %copy-start.6 = (f32[128,1024]{1,0:T(8,128)S(1)}, f32[128,1024]{1,0:T(8,128)}, u32[]{:S(2)}) copy-start(f32[128,1024]{1,0:T(8,128)} %copy-done.5) | copy-start | bytes 1572868
  900.7 154.5 %copy-start.8 = (f32[1024,128]{0,1:T(8,128)S(1)}, f32[1024,128]{0,1:T(8,128)}, u32[]{:S(2)}) copy-start(f32[1024,128]{0,1:T(8,128)} %copy-done.7) | copy-start | bytes 1572868
  1016.1 0.7 copy-start.14
Sparse Core Ops, SparseCore 0:
  10.5 48.2 all-reduce.8
  108.9 114.7 all-reduce.10
  296.9 111.1 all-reduce.12
  414.3 110.4 all-reduce.14
  598.5 111.1 all-reduce.16
  715.8 110.4 all-reduce.18
  900.9 111.1 all-reduce.20
where the time goes:
time: 1070 us; the launch traced here: 1060 us
  waiting for transfers between devices  747 us (70%)
  other arithmetic  211 us (20%)
  matrix products  53.8 us (5%)
  local copies, waits for them, and re-layouts  27.5 us (3%)
  between operations  19.2 us (2%)
    psum x6, waiting for transfers between devices, layer_total(): return lax.psum(value, 'pipe')  669 us
    another operation x20, other arithmetic, orthonormal(): lower = jnp.linalg.cholesky(total(mm(block.T, block)))  103 us
    another operation x7, other arithmetic, orthonormal(): lax.linalg.triangular_solve(lower, block, left_side=False, lower=True, tr...  64.6 us
    psum x1, waiting for transfers between devices, shards(): both = lax.psum(jnp.concatenate([left_part, right_part], axis=1), 'tensor')  48.4 us
    another operation x7, other arithmetic, reduce_plain(): lower = jnp.linalg.cholesky(mm(weights.T, weights))  34.8 us
    dot_general x10, matrix products, mm(): return jnp.matmul(a, b, precision=lax.Precision.HIGHEST)  30.7 us
    ppermute x2, waiting for transfers between devices, from_partner(): return lax.ppermute(block, axis, route)  29.7 us
  transfers between devices with their start and end apart: 9, of which 9 were waited for; matrix products, arithmetic and copies ran while one was open for 0% of the time, Pallas kernels for 0%

commit v1 on v0

--- a/solution.py
+++ b/solution.py
@@ -23,7 +23,11 @@
 
 
 def layer_total(value):
-    return lax.psum(value, "pipe")
+
+    def chains_take(patch):
+        return jnp.sum(jax.lax.all_gather(patch, "pipe"), axis=0)
+
+    return chains_take(value)
 
 
 def orthonormal(block, total):

time: 1070 us -> 708 us (0.66)
  waiting for transfers between devices: 747 us -> 369 us
  other arithmetic: 211 us -> 232 us
    psum x6 -> x0, waiting for transfers between devices: 669 us -> none  [layer_total(): return lax.psum(value, 'pipe')]
    all_gather x0 -> x6, waiting for transfers between devices: none -> 291 us  [chains_take(): return jnp.sum(jax.lax.all_gather(patch, 'pipe'), axis=0)]
    reduce_sum x0 -> x6, other arithmetic: none -> 21 us  [chains_take(): return jnp.sum(jax.lax.all_gather(patch, 'pipe'), axis=0)]
where the time goes in v1:
time: 708 us; the launch traced here: 700 us
  waiting for transfers between devices  369 us (52%)
  other arithmetic  232 us (33%)
  matrix products  49.9 us (7%)
  local copies, waits for them, and re-layouts  24.5 us (3%)
  between operations  19.4 us (3%)
    all_gather x6, waiting for transfers between devices, chains_take(): return jnp.sum(jax.lax.all_gather(patch, 'pipe'), axis=0)  291 us
    another operation x20, other arithmetic, orthonormal(): lower = jnp.linalg.cholesky(total(mm(block.T, block)))  103 us
    another operation x7, other arithmetic, orthonormal(): lax.linalg.triangular_solve(lower, block, left_side=False, lower=True, tr...  64.6 us
    psum x1, waiting for transfers between devices, shards(): both = lax.psum(jnp.concatenate([left_part, right_part], axis=1), 'tensor')  48.4 us
    another operation x7, other arithmetic, reduce_plain(): lower = jnp.linalg.cholesky(mm(weights.T, weights))  34.8 us
    ppermute x2, waiting for transfers between devices, from_partner(): return lax.ppermute(block, axis, route)  29.6 us
    dot_general x10, matrix products, mm(): return jnp.matmul(a, b, precision=lax.Precision.HIGHEST)  28.2 us
    reduce_sum x6, other arithmetic, chains_take(): return jnp.sum(jax.lax.all_gather(patch, 'pipe'), axis=0)  21 us
  transfers between devices with their start and end apart: 9, of which 9 were waited for; matrix products, arithmetic and copies ran while one was open for 0% of the time, Pallas kernels for 0%

profile of v1, /device:TPU:1, one launch (start us, length us, event | category | flops | bytes accessed | tf_op | source)
XLA Modules:
  0.0 700.2 jit_solution(6892811302131039061)
XLA Ops:
  10.4 48.4 %all-reduce.3.cloned.1.call-done = f32[512,64]{0,1:T(8,128)} async-done(((f32[512,64]{0,1:T(8,128)}), f32[512,64]{0,1:T(8,128)}) %all-reduce.3.cloned.1.call-update) | async-done | bytes 131088 | tf_op jit(solution)/shard_map/psum | solution.py:61
  66.0 9.5 %collective-permute-done = f32[1024,128]{1,0:T(8,128)S(1)} collective-permute-done((f32[1024,128]{1,0:T(8,128)S(1)}, f32[1024,128]{1,0:T(8,128)S(1)}, u32[]{:S(2)}, u32[]{:S(2)}) %collective-permute-start) | collective-permute-done | bytes 524320 | tf_op jit(solution)/shard_map/ppermute | solution.py:18
  79.6 20.0 %collective-permute-done.1 = f32[1024,256]{1,0:T(8,128)} collective-permute-done((f32[1024,256]{1,0:T(8,128)S(1)}, f32[1024,256]{1,0:T(8,128)}, u32[]{:S(2)}, u32[]{:S(2)}) %collective-permute-start.1) | collective-permute-done | bytes 1048608 | tf_op jit(solution)/shard_map/ppermute | solution.py:18
  104.5 46.9 %all-gather.13.cloned.1.call-done = f32[4096,256]{1,0:T(8,128)} async-done(((f32[256,256]{1,0:T(8,128)}), f32[4096,256]{1,0:T(8,128)}) %all-gather.13.cloned.1.call-update) | async-done | bytes 4194320 | tf_op jit(solution)/shard_map/all_gather | solution.py:28
  156.4 11.7 %cholesky.214 = f32[128,128]{1,0:T(8,128)S(1)} custom-call(f32[128,128]{1,0:T(8,128)S(1)} %cholesky.346), custom_call_target="Cholesky" | custom-call | tf_op jit(solution)/shard_map/jit(cholesky)/cholesky | solution.py:34
  168.2 9.8 %custom-call.16 = f32[1,128,128]{1,2,0:T(8,128)S(1)} custom-call(f32[1,128,128]{2,1,0:T(8,128)S(1)} %get-tuple-element.79), custom_call_target="InvertDiagBlocksLowerTriangular" | custom-call | tf_op jit(solution)/shard_map/jit(cholesky)/cholesky | solution.py:34
  180.1 11.7 %cholesky.231 = f32[128,128]{1,0:T(8,128)S(1)} custom-call(f32[128,128]{1,0:T(8,128)S(1)} %convolution_subtract_fusion.3), custom_call_target="Cholesky" | custom-call | tf_op jit(solution)/shard_map/jit(cholesky)/cholesky | solution.py:34
  194.9 4.3 while.6
  199.9 20.5 %custom-call.17 = f32[2,128,128]{1,2,0:T(8,128)S(1)} custom-call(f32[2,128,128]{2,1,0:T(8,128)} %copy-done.15), custom_call_target="InvertDiagBlocksLowerTriangular" | custom-call | tf_op jit(solution)/shard_map/triangular_solve/custom-call.0 | solution.py:35
  222.7 4.3 fusion.10
  227.0 54.5 %all-gather.15.cloned.1.call-done = f32[8192,256]{1,0:T(8,128)} async-done(((f32[512,256]{1,0:T(8,128)}), f32[8192,256]{1,0:T(8,128)}) %all-gather.15.cloned.1.call-update) | async-done | bytes 8388624 | tf_op jit(solution)/shard_map/all_gather | solution.py:28
  281.5 4.8 reduce_sum.55
  292.2 40.1 %all-gather.17.cloned.1.call-done = f32[4096,256]{1,0:T(8,128)} async-done(((f32[256,256]{1,0:T(8,128)}), f32[4096,256]{1,0:T(8,128)}) %all-gather.17.cloned.1.call-update) | async-done | bytes 4194320 | tf_op jit(solution)/shard_map/all_gather | solution.py:28
  337.3 11.7 %cholesky.248 = f32[128,128]{1,0:T(8,128)S(1)} custom-call(f32[128,128]{1,0:T(8,128)S(1)} %cholesky.349), custom_call_target="Cholesky" | custom-call | tf_op jit(solution)/shard_map/jit(cholesky)/cholesky | solution.py:34
  349.1 9.8 %custom-call.18 = f32[1,128,128]{1,2,0:T(8,128)S(1)} custom-call(f32[1,128,128]{2,1,0:T(8,128)S(1)} %get-tuple-element.75), custom_call_target="InvertDiagBlocksLowerTriangular" | custom-call | tf_op jit(solution)/shard_map/jit(cholesky)/cholesky | solution.py:34
  361.1 11.7 %cholesky.265 = f32[128,128]{1,0:T(8,128)S(1)} custom-call(f32[128,128]{1,0:T(8,128)S(1)} %convolution_subtract_fusion.2), custom_call_target="Cholesky" | custom-call | tf_op jit(solution)/shard_map/jit(cholesky)/cholesky | solution.py:34
  376.5 4.2 while.7
  381.4 20.5 %custom-call.19 = f32[2,128,128]{1,2,0:T(8,128)S(1)} custom-call(f32[2,128,128]{2,1,0:T(8,128)} %copy-done.16), custom_call_target="InvertDiagBlocksLowerTriangular" | custom-call | tf_op jit(solution)/shard_map/triangular_solve/custom-call.0 | solution.py:35
  404.1 4.3 fusion.14
  408.5 54.5 %all-gather.19.cloned.1.call-done = f32[8192,256]{1,0:T(8,128)} async-done(((f32[512,256]{1,0:T(8,128)}), f32[8192,256]{1,0:T(8,128)}) %all-gather.19.cloned.1.call-update) | async-done | bytes 8388624 | tf_op jit(solution)/shard_map/all_gather | solution.py:28
  463.0 4.8 reduce_sum.57
  473.7 40.1 %all-gather.21.cloned.1.call-done = f32[4096,256]{1,0:T(8,128)} async-done(((f32[256,256]{1,0:T(8,128)}), f32[4096,256]{1,0:T(8,128)}) %all-gather.21.cloned.1.call-update) | async-done | bytes 4194320 | tf_op jit(solution)/shard_map/all_gather | solution.py:28
  518.8 11.7 %cholesky.282 = f32[128,128]{1,0:T(8,128)S(1)} custom-call(f32[128,128]{1,0:T(8,128)S(1)} %cholesky.352), custom_call_target="Cholesky" | custom-call | tf_op jit(solution)/shard_map/jit(cholesky)/cholesky | solution.py:34
  530.6 9.8 %custom-call.20 = f32[1,128,128]{1,2,0:T(8,128)S(1)} custom-call(f32[1,128,128]{2,1,0:T(8,128)S(1)} %get-tuple-element.71), custom_call_target="InvertDiagBlocksLowerTriangular" | custom-call | tf_op jit(solution)/shard_map/jit(cholesky)/cholesky | solution.py:34
  542.6 11.7 %cholesky.299 = f32[128,128]{1,0:T(8,128)S(1)} custom-call(f32[128,128]{1,0:T(8,128)S(1)} %convolution_subtract_fusion.1), custom_call_target="Cholesky" | custom-call | tf_op jit(solution)/shard_map/jit(cholesky)/cholesky | solution.py:34
  558.0 4.1 while.8
  562.7 20.7 %custom-call.21 = f32[2,128,128]{1,2,0:T(8,128)S(1)} custom-call(f32[2,128,128]{2,1,0:T(8,128)} %copy-done.17), custom_call_target="InvertDiagBlocksLowerTriangular" | custom-call | tf_op jit(solution)/shard_map/triangular_solve/custom-call.0 | solution.py:35
  586.5 4.2 fusion.19
  590.8 54.6 %all-gather.23.cloned.1.call-done = f32[8192,256]{1,0:T(8,128)} async-done(((f32[512,256]{1,0:T(8,128)}), f32[8192,256]{1,0:T(8,128)}) %all-gather.23.cloned.1.call-update) | async-done | bytes 8388624 | tf_op jit(solution)/shard_map/all_gather | solution.py:28
  652.9 11.7 %cholesky.316 = f32[128,128]{1,0:T(8,128)S(1)} custom-call(f32[128,128]{1,0:T(8,128)S(1)} %cholesky.355), custom_call_target="Cholesky" | custom-call | tf_op jit(solution)/shard_map/jit(cholesky)/cholesky | solution.py:43
  664.6 10.0 %custom-call.22 = f32[1,128,128]{1,2,0:T(8,128)S(1)} custom-call(f32[1,128,128]{2,1,0:T(8,128)S(1)} %get-tuple-element.67), custom_call_target="InvertDiagBlocksLowerTriangular" | custom-call | tf_op jit(solution)/shard_map/jit(cholesky)/cholesky | solution.py:43
  676.8 11.7 %cholesky.333 = f32[128,128]{1,0:T(8,128)S(1)} custom-call(f32[128,128]{1,0:T(8,128)S(1)} %convolution_subtract_fusion), custom_call_target="Cholesky" | custom-call | tf_op jit(solution)/shard_map/jit(cholesky)/cholesky | solution.py:43
  (152 shorter events, 94.3 us)
Async XLA Ops:
  6.5 1.7 copy-start
  6.5 52.3 %all-reduce.3.cloned.1.call-start = ((), (), s32[]{:S(2)}) async-start(), calls=%async_computation | async-start | bytes 262144 | tf_op jit(solution)/shard_map/psum | solution.py:61
  6.5 2.4 copy-start.7
  10.4 141.0 %all-gather.13.cloned.1.call-start = ((), (), s32[]{:S(2)}) async-start(), calls=%async_computation.1 | async-start | bytes 4456448 | tf_op jit(solution)/shard_map/all_gather | solution.py:28
  64.7 1.3 copy-start.6
  64.7 10.8 %collective-permute-start = (f32[1024,128]{1,0:T(8,128)S(1)}, f32[1024,128]{1,0:T(8,128)S(1)}, u32[]{:S(2)}, u32[]{:S(2)}) collective-permute-start(f32[1024,128]{1,0:T(8,128)S(1)} %bitcast.179), channel_id=1, source_target_pairs={{0,4},{4,0},{8,12},{12,8},{1,5},{5,1},{9,13},{13,9},{2,6},{6,2},{1... | collective-permute-start | bytes 1572872 | tf_op jit(solution)/shard_map/ppermute | solution.py:18
  76.8 22.8 %collective-permute-start.1 = (f32[1024,256]{1,0:T(8,128)S(1)}, f32[1024,256]{1,0:T(8,128)}, u32[]{:S(2)}, u32[]{:S(2)}) collective-permute-start(f32[1024,256]{1,0:T(8,128)S(1)} %maximum_select_fusion.1), channel_id=1, source_target_pairs={{0,8},{8,0},{4,12},{12,4},{1,9},{9,1},{5,13},{13,5},{2,10},{10,2},... | collective-permute-start | bytes 3145736 | tf_op jit(solution)/shard_map/ppermute | solution.py:18
  104.2 177.3 %all-gather.15.cloned.1.call-start = ((), (), s32[]{:S(2)}) async-start(), calls=%async_computation.2 | async-start | bytes 8912896 | tf_op jit(solution)/shard_map/all_gather | solution.py:28
  155.7 0.7 copy-start.12
  191.9 2.0 copy-start.8
  199.2 0.6 copy-start.15
  227.0 105.4 %all-gather.17.cloned.1.call-start = ((), (), s32[]{:S(2)}) async-start(), calls=%async_computation.3 | async-start | bytes 4456448 | tf_op jit(solution)/shard_map/all_gather | solution.py:28
  291.8 171.3 %all-gather.19.cloned.1.call-start = ((), (), s32[]{:S(2)}) async-start(), calls=%async_computation.4 | async-start | bytes 8912896 | tf_op jit(solution)/shard_map/all_gather | solution.py:28
  336.6 0.7 copy-start.13
  372.8 2.6 copy-start.9
  380.7 0.6 copy-start.16
  408.5 105.4 %all-gather.21.cloned.1.call-start = ((), (), s32[]{:S(2)}) async-start(), calls=%async_computation.5 | async-start | bytes 4456448 | tf_op jit(solution)/shard_map/all_gather | solution.py:28
  473.3 172.1 %all-gather.23.cloned.1.call-start = ((), (), s32[]{:S(2)}) async-start(), calls=%async_computation.6 | async-start | bytes 8912896 | tf_op jit(solution)/shard_map/all_gather | solution.py:28
  518.1 0.7 copy-start.14
  554.3 2.6 copy-start.10
  562.0 0.6 copy-start.17
  584.0 1.7 copy-start.2
  585.6 0.8 copy-start.4
  649.3 42.0 %copy-start.3 = (f32[128,1024]{1,0:T(8,128)S(1)}, f32[128,1024]{1,0:T(8,128)}, u32[]{:S(2)}) copy-start(f32[128,1024]{1,0:T(8,128)} %copy-done.2) | copy-start | bytes 1572868
  649.3 42.0 %copy-start.5 = (f32[1024,128]{0,1:T(8,128)S(1)}, f32[1024,128]{0,1:T(8,128)}, u32[]{:S(2)}) copy-start(f32[1024,128]{0,1:T(8,128)} %copy-done.4) | copy-start | bytes 1572868
  650.3 42.8 %copy-start.1 = (bf16[1,512,2048]{2,1,0:T(8,128)(2,1)S(1)}, bf16[1,512,2048]{2,1,0:T(8,128)(2,1)}, u32[]{:S(2)}) copy-start(bf16[1,512,2048]{2,1,0:T(8,128)(2,1)} %param.7) | copy-start | bytes 6291460
  652.2 0.7 copy-start.11
Sparse Core Ops, SparseCore 0:
  10.5 48.2 all-reduce.2
  104.4 46.9 all-gather.12
  227.1 54.4 all-gather.14
  291.9 40.4 all-gather.16
  408.6 54.4 all-gather.18
  473.4 40.4 all-gather.20
  590.9 54.3 all-gather.22
